TPU v7x, 32 devices: a whole 2x2x4 slice. The times are simulated.
32 devices in a mesh: dp: 2 (over x), row: 4 (over z), col: 4 (over y, core).
Axes of the slice: x: 2, y: 2, z: 4, core: 2. Of those that a mesh axis runs over, the one named last changes fastest.
Arguments:
- layer_input: bfloat16 [1536, 6144], P(('dp', 'col'), 'row'), may hold values from -125 to 125
- grad_output: bfloat16 [1536, 6144], P(('dp', 'col'), 'row'), may hold values from -6 to 6
- pre_activation: bfloat16 [1536, 24576], P(('dp', 'row'), 'col'), may hold values from -6 to 6
- norm_gain_vector: float32 [6144], P('row'), may hold values from 0.5 to 1.5
- up_weight: bfloat16 [6144, 24576], P('row', 'col'), may hold values from -0.078125 to 0.078125
- down_weight: bfloat16 [24576, 6144], P('col', 'row'), may hold values from -0.0390625 to 0.0390625
Outputs:
- input_gradient: float32 [1536, 6144], P(('dp', 'col'), 'row')
- grad_up: float32 [6144, 24576], P(('row', 'dp'), 'col')
- grad_down: float32 [24576, 6144], P('col', ('row', 'dp'))
- grad_bias: float32 [24576], P('col')
- gain_gradient: float32 [6144], P('row')
All inputs are finite; a program needn't handle non-finite values.
Results may differ from a plain program's by a relative error of at most 0.0055.
Values may be sent and summed in bfloat16 or wider, within the bound.
A program may use at most 256 MiB of HBM per device.

v0:
```python
import jax
import jax.numpy as jnp
from jax import lax
from jax.sharding import PartitionSpec as P

MODEL_WIDTH = 6144


epsilon = 1e-06


def gelu_parts(pre_float):
    normal_cdf = 0.5 * (1.0 + lax.erf(pre_float * 0.7071067811865476))
    normal_pdf = jnp.exp(-0.5 * pre_float * pre_float) * 0.3989422804014327
    return (pre_float * normal_cdf, normal_cdf + pre_float * normal_pdf)


def contract_last(left, right):
    return lax.dot_general(
        left, right, (((1,), (1,)), ((), ())), preferred_element_type=jnp.float32
    )


def contract_first(left, right):
    return lax.dot_general(
        left, right, (((0,), (0,)), ((), ())), preferred_element_type=jnp.float32
    )


def per_device(layer_input, grad_output, pre_activation, norm_gain_vector, up_weight, down_weight):
    input_single_precision = layer_input.astype(jnp.float32)
    sum_rows, square_rows = lax.psum(
        (
            jnp.sum(input_single_precision, axis=1),
            jnp.sum(input_single_precision * input_single_precision, axis=1),
        ),
        "row",
    )
    row_average = sum_rows / MODEL_WIDTH
    reciprocal_deviation = 1.0 / jnp.sqrt(
        square_rows / MODEL_WIDTH - row_average * row_average + epsilon
    )
    centered_standardized = (input_single_precision - row_average[:, None]) * reciprocal_deviation[
        :, None
    ]
    normalized_rows = (centered_standardized * norm_gain_vector[None, :]).astype(jnp.bfloat16)
    normed_all, grad_all = (
        lax.all_gather(normalized_rows, "col", axis=0, tiled=True),
        lax.all_gather(grad_output, "col", axis=0, tiled=True),
    )
    block = grad_all
    grad_act = lax.psum_scatter(
        contract_last(block, down_weight), "row", scatter_dimension=0, tiled=True
    )
    gelu_value, gelu_slope = gelu_parts(pre_activation.astype(jnp.float32))
    grad_hidden = (grad_act * gelu_slope).astype(jnp.bfloat16)
    activation = gelu_value.astype(jnp.bfloat16)
    grad_bias = lax.psum(jnp.sum(grad_hidden.astype(jnp.float32), axis=0), ("dp", "row"))
    hidden_all, activ_all = (
        lax.all_gather(grad_hidden, "row", axis=0, tiled=True),
        lax.all_gather(activation, "row", axis=0, tiled=True),
    )
    block = hidden_all
    normalized_gradient = lax.psum_scatter(
        contract_last(block, up_weight), "col", scatter_dimension=0, tiled=True
    )
    gain_scaled_rows = normalized_gradient * norm_gain_vector[None, :]
    leading_total_sum, trailing_total_sum = lax.psum(
        (
            jnp.sum(gain_scaled_rows, axis=1),
            jnp.sum(gain_scaled_rows * centered_standardized, axis=1),
        ),
        "row",
    )
    input_gradient = reciprocal_deviation[:, None] * (
        gain_scaled_rows
        - leading_total_sum[:, None] / MODEL_WIDTH
        - centered_standardized * (trailing_total_sum[:, None] / MODEL_WIDTH)
    )
    gain_gradient = lax.psum(
        jnp.sum(normalized_gradient * centered_standardized, axis=0), ("dp", "col")
    )
    local_up = contract_first(normed_all, hidden_all)
    local_down = contract_first(activ_all, grad_all)
    grad_up, grad_down = (
        lax.psum_scatter(local_up, "dp", scatter_dimension=0, tiled=True),
        lax.psum_scatter(local_down, "dp", scatter_dimension=1, tiled=True),
    )
    return (input_gradient, grad_up, grad_down, grad_bias, gain_gradient)


def solution(mesh):
    placed = (
        P(("dp", "col"), "row"),
        P(("dp", "col"), "row"),
        P(("dp", "row"), "col"),
        P("row"),
        P("row", "col"),
        P("col", "row"),
    )
    return jax.shard_map(
        per_device,
        mesh=mesh,
        in_specs=placed,
        out_specs=(
            P(("dp", "col"), "row"),
            P(("row", "dp"), "col"),
            P("col", ("row", "dp")),
            P("col"),
            P("row"),
        ),
        check_vma=False,
    )
```

profile of v0, /device:TPU:0, one launch (start us, length us, event | category | flops | bytes accessed | tf_op | source)
XLA Modules:
  0.0 1647.4 jit_solution(15103876984587123536)
XLA Ops:
  7.2 0.7 all-gather.5.cloned.1.call-update
  7.9 28.4 %all-gather.5.cloned.1.call-done = bf16[768,1536]{1,0:T(8,128)(2,1)} async-done(((bf16[192,1536]{1,0:T(8,128)(2,1)}), bf16[768,1536]{1,0:T(8,128)(2,1)}) %all-gather.5.cloned.1.call-update) | async-done | bytes 2359312 | tf_op jit(solution)/shard_map/all_gather | solution.py:49
  36.3 21.4 %fusion.21 = f32[768,6144]{1,0:T(8,128)} fusion(bf16[768,1536]{1,0:T(8,128)(2,1)} %all-gather.5.cloned.1.call-done, bf16[6144,1536]{1,0:T(8,128)(2,1)} %param.11), kind=kOutput, calls=%fused_computation.34 | convolution fusion | flops 14495514624 | bytes 40108032 | tf_op jit(solution)/shard_map/dot_general | solution.py:19
  57.8 314.0 %reduce-scatter.5.cloned.1.call-done = f32[192,6144]{1,0:T(8,128)} async-done(((f32[768,6144]{1,0:T(8,128)}), f32[192,6144]{1,0:T(8,128)}) %reduce-scatter.5.cloned.1.call-update) | async-done | bytes 4718608 | tf_op jit(solution)/shard_map/reduce_scatter | solution.py:52
  371.9 5.6 convert_reduce_fusion
  377.6 167.8 %all-gather.7.cloned.1.call-done = bf16[768,6144]{1,0:T(8,128)(2,1)} async-done(((bf16[192,6144]{1,0:T(8,128)(2,1)}), bf16[768,6144]{1,0:T(8,128)(2,1)}) %all-gather.7.cloned.1.call-update) | async-done | bytes 9437200 | tf_op jit(solution)/shard_map/all_gather | solution.py:60
  545.4 21.2 %fusion.22 = f32[768,1536]{1,0:T(8,128)} fusion(bf16[768,6144]{1,0:T(8,128)(2,1)} %all-gather.7.cloned.1.call-done, bf16[1536,6144]{1,0:T(8,128)(2,1)} %param.10), kind=kOutput, calls=%fused_computation.35 | convolution fusion | flops 14495514624 | bytes 33030144 | tf_op jit(solution)/shard_map/dot_general | solution.py:19
  566.6 0.5 all-gather.11.cloned.1.call-update
  567.2 0.4 copy-done
  567.6 0.2 fusion.9
  567.9 8.6 all-reduce.1
  576.5 36.3 %reduce-scatter.7.cloned.1.call-done = f32[192,1536]{1,0:T(8,128)} async-done(((f32[768,1536]{1,0:T(8,128)}), f32[192,1536]{1,0:T(8,128)}) %reduce-scatter.7.cloned.1.call-update) | async-done | bytes 1179664 | tf_op jit(solution)/shard_map/reduce_scatter | solution.py:64
  612.9 2.6 fusion.19
  615.5 0.2 reduce-scatter.11.cloned.1.call-start
  615.7 165.9 %all-gather.11.cloned.1.call-done = bf16[768,6144]{1,0:T(8,128)(2,1)} async-done(((bf16[192,6144]{1,0:T(8,128)(2,1)}), bf16[768,6144]{1,0:T(8,128)(2,1)}) %all-gather.11.cloned.1.call-update) | async-done | bytes 9437200 | tf_op jit(solution)/shard_map/all_gather | solution.py:61
  781.7 22.6 %fusion.24 = f32[6144,1536]{1,0:T(8,128)} fusion(bf16[768,6144]{1,0:T(8,128)(2,1)} %all-gather.11.cloned.1.call-done, bf16[768,1536]{1,0:T(8,128)(2,1)S(1)} %copy-done.4), kind=kOutput, calls=%fused_computation.37 | convolution fusion | flops 14495514624 | bytes 49545216 | tf_op jit(solution)/shard_map/dot_general | solution.py:25
  804.3 1.6 all-gather.9.cloned.1.call-done
  805.9 22.8 %fusion.23 = f32[1536,6144]{1,0:T(8,128)} fusion(bf16[768,1536]{1,0:T(8,128)(2,1)} %all-gather.9.cloned.1.call-done, bf16[768,6144]{1,0:T(8,128)(2,1)} %all-gather.7.cloned.1.call-done), kind=kOutput, calls=%fused_computation.36 | convolution fusion | flops 14495514624 | bytes 49545216 | tf_op jit(solution)/shard_map/dot_general | solution.py:25
  828.8 38.7 %psum.46 = f32[6144]{0:T(1024)} all-reduce(f32[6144]{0:T(1024)S(1)} %get-tuple-element.14), channel_id=1, replica_groups=mesh['dp'=2,'row'=4,'col'=4] {'dp','row'}, use_global_device_ids=true, to_apply=%region_13.0 | all-reduce | flops 6144 | bytes 49152 | tf_op jit(solution)/shard_map/psum | solution.py:58
  867.5 8.3 all-reduce
  875.8 13.9 psum.47
  889.7 1.4 fusion.17
  891.1 332.6 %reduce-scatter.11.cloned.1.call-done = f32[6144,768]{1,0:T(8,128)} async-done(((f32[6144,1536]{1,0:T(8,128)}), f32[6144,768]{1,0:T(8,128)}) %reduce-scatter.11.cloned.1.call-update) | async-done | bytes 18874384 | tf_op jit(solution)/shard_map/reduce_scatter | solution.py:87
  1223.8 416.8 %reduce-scatter.9.cloned.1.call-done = f32[768,6144]{1,0:T(8,128)} async-done(((f32[1536,6144]{1,0:T(8,128)}), f32[768,6144]{1,0:T(8,128)}) %reduce-scatter.9.cloned.1.call-update) | async-done | bytes 18874384 | tf_op jit(solution)/shard_map/reduce_scatter | solution.py:86
  (24 shorter events, 0.4 us)
Async XLA Ops:
  7.2 29.2 %all-gather.5.cloned.1.call-start = ((), (), s32[]{:S(2)}) async-start(), calls=%async_computation.4 | async-start | bytes 2949120 | tf_op jit(solution)/shard_map/all_gather | solution.py:49
  7.9 364.0 %reduce-scatter.5.cloned.1.call-start = ((), (), s32[]{:S(2)}) async-start(), calls=%async_computation.5 | async-start | bytes 23592960 | tf_op jit(solution)/shard_map/reduce_scatter | solution.py:52
  57.7 314.1 %copy-start.2 = (bf16[192,6144]{1,0:T(8,128)(2,1)S(1)}, bf16[192,6144]{1,0:T(8,128)(2,1)}, u32[]{:S(2)}) copy-start(bf16[192,6144]{1,0:T(8,128)(2,1)} %param.8) | copy-start | bytes 7077892
  57.8 487.6 %all-gather.7.cloned.1.call-start = ((), (), s32[]{:S(2)}) async-start(), calls=%async_computation.6 | async-start | bytes 11796480 | tf_op jit(solution)/shard_map/all_gather | solution.py:60
  377.5 235.3 %reduce-scatter.7.cloned.1.call-start = ((), (), s32[]{:S(2)}) async-start(), calls=%async_computation.7 | async-start | bytes 5898240 | tf_op jit(solution)/shard_map/reduce_scatter | solution.py:64
  566.5 1.1 copy-start
  566.5 46.3 %copy-start.3 = (f32[1536]{0:T(1024)S(1)}, f32[1536]{0:T(1024)}, u32[]{:S(2)}) copy-start(f32[1536]{0:T(1024)} %param.9) | copy-start | bytes 18436
  566.5 215.1 %copy-start.4 = (bf16[768,1536]{1,0:T(8,128)(2,1)S(1)}, bf16[768,1536]{1,0:T(8,128)(2,1)}, u32[]{:S(2)}) copy-start(bf16[768,1536]{1,0:T(8,128)(2,1)} %all-gather.5.cloned.1.call-done) | copy-start | bytes 7077892
  566.6 215.1 %all-gather.11.cloned.1.call-start = ((), (), s32[]{:S(2)}) async-start(), calls=%async_computation.10 | async-start | bytes 11796480 | tf_op jit(solution)/shard_map/all_gather | solution.py:61
  567.2 238.7 %all-gather.9.cloned.1.call-start = ((), (), s32[]{:S(2)}) async-start(), calls=%async_computation.8 | async-start | bytes 2949120 | tf_op jit(solution)/shard_map/all_gather | solution.py:48
  615.5 608.3 %reduce-scatter.11.cloned.1.call-start = ((), (), s32[]{:S(2)}) async-start(), calls=%async_computation.11 | async-start | bytes 56623104 | tf_op jit(solution)/shard_map/reduce_scatter | solution.py:87
  804.3 836.3 %reduce-scatter.9.cloned.1.call-start = ((), (), s32[]{:S(2)}) async-start(), calls=%async_computation.9 | async-start | bytes 56623104 | tf_op jit(solution)/shard_map/reduce_scatter | solution.py:86
  828.7 61.0 %copy-start.1 = (f32[192,1536]{1,0:T(8,128)S(1)}, f32[192,1536]{1,0:T(8,128)}, u32[]{:S(2)}) copy-start(f32[192,1536]{1,0:T(8,128)} %reduce-scatter.7.cloned.1.call-done) | copy-start | bytes 3538948
Sparse Core Ops, SparseCore 0:
  9.5 26.7 all-gather.4
  57.9 313.9 reduce-scatter.4
  377.6 167.6 all-gather.6
  566.7 46.1 reduce-scatter.6
  614.8 166.7 all-gather.10
  783.6 22.2 all-gather.8
  808.8 414.9 reduce-scatter.10
  1226.6 413.8 reduce-scatter.8
where the time goes:
time: 1650 us
  waiting for transfers between devices  1460 us (88%)
  matrix products  88 us (5%)
  blocking collectives  69.6 us (4%)
    reduce_scatter x1, waiting for transfers between devices, per_device(): lax.psum_scatter(local_up, 'dp', scatter_dimension=0, tiled=True)  417 us
    reduce_scatter x1, waiting for transfers between devices, per_device(): lax.psum_scatter(local_down, 'dp', scatter_dimension=1, tiled=True)  333 us
    reduce_scatter x1, waiting for transfers between devices, per_device(): lax.psum_scatter(contract_last(block, down_weight), 'row', scatter_dimens...  314 us
    all_gather x1, waiting for transfers between devices, per_device(): lax.all_gather(grad_hidden, 'row', axis=0, tiled=True)  168 us
    all_gather x1, waiting for transfers between devices, per_device(): lax.all_gather(activation, 'row', axis=0, tiled=True)  166 us
    dot_general x2, matrix products, contract_first(): lax.dot_general(left, right, (((0,), (0,)), ((), ())), preferred_element_...  45.4 us
    dot_general x2, matrix products, contract_last(): lax.dot_general(left, right, (((1,), (1,)), ((), ())), preferred_element_...  42.6 us
    psum x1, blocking collectives, per_device(): lax.psum(jnp.sum(grad_hidden.astype(jnp.float32), axis=0), ('dp', 'row'))  38.7 us
  transfers between devices with their start and end apart: 8, of which 8 were waited for; matrix products, arithmetic and copies ran while one was open for 3% of the time, Pallas kernels for 0%

commit v1 on v0

v1 whole, which is shorter than its diff:
```python
import jax
import jax.numpy as jnp
from jax import lax
from jax.sharding import PartitionSpec as P

CHUNKS = 4
epsilon = 1e-06


def gelu_parts(pre_float):
    normal_cdf = 0.5 * (1.0 + lax.erf(pre_float * 0.7071067811865476))
    normal_pdf = jnp.exp(-0.5 * pre_float * pre_float) * 0.3989422804014327
    return (pre_float * normal_cdf, normal_cdf + pre_float * normal_pdf)


def contract_last(left, right):
    return lax.dot_general(
        left, right, (((1,), (1,)), ((), ())), preferred_element_type=jnp.float32
    )


def contract_first(left, right):
    return lax.dot_general(
        left, right, (((0,), (0,)), ((), ())), preferred_element_type=jnp.float32
    )


def build(sizes):
    swap = [(0, 1), (1, 0)]
    two = sizes["dp"] == 2

    def per_device(
        layer_input, grad_output, pre_activation, norm_gain_vector, up_weight, down_weight
    ):
        model_width = layer_input.shape[1] * sizes["row"]
        hidden = pre_activation.shape[1]
        chunks = CHUNKS if hidden % (CHUNKS * 128) == 0 else 1
        step = hidden // chunks
        me = lax.axis_index("dp")
        grad_all = lax.all_gather(grad_output, "col", axis=0, tiled=True)
        x = layer_input.astype(jnp.float32)
        sum_rows, square_rows = lax.psum(
            (jnp.sum(x, axis=1), jnp.sum(x * x, axis=1)), "row"
        )
        mean = sum_rows / model_width
        inv_std = 1.0 / jnp.sqrt(square_rows / model_width - mean * mean + epsilon)
        xhat = (x - mean[:, None]) * inv_std[:, None]
        normed = (xhat * norm_gain_vector[None, :]).astype(jnp.bfloat16)
        normed_all = lax.all_gather(normed, "col", axis=0, tiled=True)

        half = layer_input.shape[1] // sizes["dp"]

        def part(array, index):
            return lax.dynamic_slice_in_dim(array, index * half, half, axis=1)

        if two:
            normed_mine, normed_other = part(normed_all, me), part(normed_all, 1 - me)
            grad_mine, grad_other = part(grad_all, me), part(grad_all, 1 - me)

        def up_of(hid):
            if not two:
                return lax.psum_scatter(
                    contract_first(normed_all, hid), "dp", scatter_dimension=0, tiled=True
                )
            away = contract_first(normed_other, hid).astype(jnp.bfloat16)
            got = lax.ppermute(away, "dp", swap)
            return contract_first(normed_mine, hid) + got.astype(jnp.float32)

        def down_of(act):
            if not two:
                return lax.psum_scatter(
                    contract_first(act, grad_all), "dp", scatter_dimension=1, tiled=True
                )
            away = contract_first(act, grad_other).astype(jnp.bfloat16)
            got = lax.ppermute(away, "dp", swap)
            return contract_first(act, grad_mine) + got.astype(jnp.float32)

        ups, downs, biases, total = [], [], [], None
        for k in range(chunks):
            cut = slice(k * step, (k + 1) * step)
            value, slope = gelu_parts(pre_activation[:, cut].astype(jnp.float32))
            grad_act = lax.psum_scatter(
                contract_last(grad_all, down_weight[cut]).astype(jnp.bfloat16),
                "row",
                scatter_dimension=0,
                tiled=True,
            )
            act_all = lax.all_gather(value.astype(jnp.bfloat16), "row", axis=0, tiled=True)
            grad_hidden = (grad_act.astype(jnp.float32) * slope).astype(jnp.bfloat16)
            hid_all = lax.all_gather(grad_hidden, "row", axis=0, tiled=True)
            downs.append(down_of(act_all))
            ups.append(up_of(hid_all))
            biases.append(jnp.sum(hid_all.astype(jnp.float32), axis=0))
            term = contract_last(hid_all, up_weight[:, cut])
            total = term if total is None else total + term
        bias = jnp.concatenate(biases)
        grad_bias = bias + lax.ppermute(bias, "dp", swap) if two else lax.psum(bias, "dp")
        grad_up = jnp.concatenate(ups, axis=1)
        grad_down = jnp.concatenate(downs, axis=0)

        grad_normed = lax.psum_scatter(
            total.astype(jnp.bfloat16), "col", scatter_dimension=0, tiled=True
        ).astype(jnp.float32)
        scaled = grad_normed * norm_gain_vector[None, :]
        first, second = lax.psum(
            (jnp.sum(scaled, axis=1), jnp.sum(scaled * xhat, axis=1)), "row"
        )
        input_gradient = inv_std[:, None] * (
            scaled - first[:, None] / model_width - xhat * (second[:, None] / model_width)
        )
        gain_gradient = lax.psum(jnp.sum(grad_normed * xhat, axis=0), ("dp", "col"))
        return (input_gradient, grad_up, grad_down, grad_bias, gain_gradient)

    return per_device


def solution(mesh):
    placed = (
        P(("dp", "col"), "row"),
        P(("dp", "col"), "row"),
        P(("dp", "row"), "col"),
        P("row"),
        P("row", "col"),
        P("col", "row"),
    )
    return jax.shard_map(
        build(dict(mesh.shape)),
        mesh=mesh,
        in_specs=placed,
        out_specs=(
            P(("dp", "col"), "row"),
            P(("row", "dp"), "col"),
            P("col", ("row", "dp")),
            P("col"),
            P("row"),
        ),
        check_vma=False,
    )
```

time: 1650 us -> 981 us (0.59)
  waiting for transfers between devices: 1460 us -> 613 us
  blocking collectives: 69.6 us -> 156 us
  matrix products: 88 us -> 147 us
  other arithmetic: 9.93 us -> 28.1 us
    reduce_scatter x4 -> x5, waiting for transfers between devices: 1100 us -> 200 us  [the longest x4 172 us: per_device(): lax.psum_scatter(contract_last(grad_all, down_weight[cut]).astype(jnp.bfl...]
    psum x4 -> x3, blocking collectives: 69.6 us -> 156 us  [the longest x1 136 us: per_device(): gain_gradient = lax.psum(jnp.sum(grad_normed * xhat, axis=0), ('dp', 'col'))]
    ppermute x0 -> x9, waiting for transfers between devices: none -> 53 us  [the longest x4 36.6 us: up_of(): got = lax.ppermute(away, 'dp', swap)]
    dot_general x2 -> x16, matrix products: 45.4 us -> 76.3 us  [contract_first(): lax.dot_general(left, right, (((0,), (0,)), ((), ())), preferred_element_...]
    dot_general x2 -> x8, matrix products: 42.6 us -> 70.4 us  [contract_last(): lax.dot_general(left, right, (((1,), (1,)), ((), ())), preferred_element_...]
    all_gather x4 -> x10, waiting for transfers between devices: 364 us -> 355 us  [the longest x4 169 us: per_device(): hid_all = lax.all_gather(grad_hidden, 'row', axis=0, tiled=True)]
  transfers between devices with their start and end apart: 8 -> 24, of which waited for: 8 -> 16; matrix products, arithmetic and copies ran while one was open for 3% -> 15% of each run, Pallas kernels for 0% -> 0%
where the time goes in v1:
time: 981 us; the launch traced here: 974 us
  waiting for transfers between devices  613 us (62%)
  blocking collectives  156 us (16%)
  matrix products  147 us (15%)
  other arithmetic  28.1 us (3%)
  between operations  14.6 us (1%)
  starting transfers between devices  12.7 us (1%)
    reduce_scatter x4, waiting for transfers between devices, per_device(): lax.psum_scatter(contract_last(grad_all, down_weight[cut]).astype(jnp.bfl...  172 us
    all_gather x4, waiting for transfers between devices, per_device(): hid_all = lax.all_gather(grad_hidden, 'row', axis=0, tiled=True)  169 us
    all_gather x4, waiting for transfers between devices, per_device(): lax.all_gather(value.astype(jnp.bfloat16), 'row', axis=0, tiled=True)  158 us
    psum x1, blocking collectives, per_device(): gain_gradient = lax.psum(jnp.sum(grad_normed * xhat, axis=0), ('dp', 'col'))  136 us
    dot_general x16, matrix products, contract_first(): lax.dot_general(left, right, (((0,), (0,)), ((), ())), preferred_element_...  76.3 us
    dot_general x8, matrix products, contract_last(): lax.dot_general(left, right, (((1,), (1,)), ((), ())), preferred_element_...  70.4 us
    ppermute x4, waiting for transfers between devices, up_of(): got = lax.ppermute(away, 'dp', swap)  36.6 us
    all_gather x1, waiting for transfers between devices, per_device(): grad_all = lax.all_gather(grad_output, 'col', axis=0, tiled=True)  28.4 us
  transfers between devices with their start and end apart: 24, of which 16 were waited for; matrix products, arithmetic and copies ran while one was open for 15% of the time, Pallas kernels for 0%

profile of v1, /device:TPU:0, one launch (start us, length us, event | category | flops | bytes accessed | tf_op | source)
XLA Modules:
  0.0 974.2 jit_solution(11959575978303377760)
XLA Ops:
  7.9 28.4 %all-gather.11.cloned.1.call-done = bf16[768,1536]{1,0:T(8,128)(2,1)} async-done(((bf16[192,1536]{1,0:T(8,128)(2,1)}), bf16[768,1536]{1,0:T(8,128)(2,1)}) %all-gather.11.cloned.1.call-update) | async-done | bytes 2359312 | tf_op jit(solution)/shard_map/all_gather | solution.py:40
  36.3 8.3 fusion.22
  68.8 23.7 %reduce-scatter.10.cloned.1.call-done = bf16[192,1536]{1,0:T(8,128)(2,1)} async-done(((bf16[768,1536]{1,0:T(8,128)(2,1)}), bf16[192,1536]{1,0:T(8,128)(2,1)}) %reduce-scatter.10.cloned.1.call-update) | async-done | bytes 589840 | tf_op jit(solution)/shard_map/reduce_scatter | solution.py:82
  92.5 50.0 %reduce-scatter.12.cloned.1.call-done = bf16[192,1536]{1,0:T(8,128)(2,1)} async-done(((bf16[768,1536]{1,0:T(8,128)(2,1)}), bf16[192,1536]{1,0:T(8,128)(2,1)}) %reduce-scatter.12.cloned.1.call-update) | async-done | bytes 589840 | tf_op jit(solution)/shard_map/reduce_scatter | solution.py:82
  142.5 49.3 %reduce-scatter.6.cloned.1.call-done = bf16[192,1536]{1,0:T(8,128)(2,1)} async-done(((bf16[768,1536]{1,0:T(8,128)(2,1)}), bf16[192,1536]{1,0:T(8,128)(2,1)}) %reduce-scatter.6.cloned.1.call-update) | async-done | bytes 589840 | tf_op jit(solution)/shard_map/reduce_scatter | solution.py:82
  191.8 49.3 %reduce-scatter.8.cloned.1.call-done = bf16[192,1536]{1,0:T(8,128)(2,1)} async-done(((bf16[768,1536]{1,0:T(8,128)(2,1)}), bf16[192,1536]{1,0:T(8,128)(2,1)}) %reduce-scatter.8.cloned.1.call-update) | async-done | bytes 589840 | tf_op jit(solution)/shard_map/reduce_scatter | solution.py:82
  252.2 44.1 %all-gather.13.cloned.1.call-done = bf16[768,1536]{1,0:T(8,128)(2,1)} async-done(((bf16[192,1536]{1,0:T(8,128)(2,1)}), bf16[768,1536]{1,0:T(8,128)(2,1)}) %all-gather.13.cloned.1.call-update) | async-done | bytes 2359312 | tf_op jit(solution)/shard_map/all_gather | solution.py:90
  296.3 9.1 fusion.12
  305.4 41.8 %all-gather.17.cloned.1.call-done = bf16[768,1536]{1,0:T(8,128)(2,1)} async-done(((bf16[192,1536]{1,0:T(8,128)(2,1)}), bf16[768,1536]{1,0:T(8,128)(2,1)}) %all-gather.17.cloned.1.call-update) | async-done | bytes 2359312 | tf_op jit(solution)/shard_map/all_gather | solution.py:90
  347.3 9.1 fusion.4
  356.3 41.3 %all-gather.15.cloned.1.call-done = bf16[768,1536]{1,0:T(8,128)(2,1)} async-done(((bf16[192,1536]{1,0:T(8,128)(2,1)}), bf16[768,1536]{1,0:T(8,128)(2,1)}) %all-gather.15.cloned.1.call-update) | async-done | bytes 2359312 | tf_op jit(solution)/shard_map/all_gather | solution.py:90
  397.6 9.0 fusion.8
  406.6 41.3 %all-gather.19.cloned.1.call-done = bf16[768,1536]{1,0:T(8,128)(2,1)} async-done(((bf16[192,1536]{1,0:T(8,128)(2,1)}), bf16[768,1536]{1,0:T(8,128)(2,1)}) %all-gather.19.cloned.1.call-update) | async-done | bytes 2359312 | tf_op jit(solution)/shard_map/all_gather | solution.py:90
  447.9 12.6 %add_convert_fusion = bf16[768,1536]{1,0:T(8,128)(2,1)} fusion(f32[768,1536]{1,0:T(8,128)} %fusion.4, f32[768,1536]{1,0:T(8,128)} %fusion.12, f32[768,1536]{1,0:T(8,128)} %fusion.8, bf16[768,1536]{1,0:T(8,128)(2,1)} %all-gather.19.cloned.1.call-done, bf16[1536,6144]{1,0:T(8,128)(2,1)} %param.10), kind=kOutput, calls=%fused_computation.14 | convolution fusion | flops 3628597248 | bytes 23592960 | tf_op jit(solution)/shard_map/dot_general | solution.py:17
  461.9 10.3 %all-reduce.1 = (f32[192]{0:T(256)S(1)}, f32[192]{0:T(256)S(1)}) all-reduce(f32[192]{0:T(256)S(1)} %get-tuple-element.9, f32[192]{0:T(256)S(1)} %get-tuple-element.8), channel_id=1, replica_groups=mesh['dp'=2,'row'=4,'col'=4] {'row'}, use_global_device_ids=true, to_apply=%region_3.0 | all-reduce | flops 384 | bytes 3072 | tf_op jit(solution)/shard_map/psum | solution.py:42
  472.2 26.2 %all-gather.29.cloned.1.call-done = bf16[768,1536]{1,0:T(8,128)(2,1)} async-done(((bf16[192,1536]{1,0:T(8,128)(2,1)}), bf16[768,1536]{1,0:T(8,128)(2,1)}) %all-gather.29.cloned.1.call-update) | async-done | bytes 2359312 | tf_op jit(solution)/shard_map/all_gather | solution.py:88
  505.0 43.8 %all-gather.27.cloned.1.call-done = bf16[768,1536]{1,0:T(8,128)(2,1)} async-done(((bf16[192,1536]{1,0:T(8,128)(2,1)}), bf16[768,1536]{1,0:T(8,128)(2,1)}) %all-gather.27.cloned.1.call-update) | async-done | bytes 2359312 | tf_op jit(solution)/shard_map/all_gather | solution.py:88
  555.3 43.6 %all-gather.25.cloned.1.call-done = bf16[768,1536]{1,0:T(8,128)(2,1)} async-done(((bf16[192,1536]{1,0:T(8,128)(2,1)}), bf16[768,1536]{1,0:T(8,128)(2,1)}) %all-gather.25.cloned.1.call-update) | async-done | bytes 2359312 | tf_op jit(solution)/shard_map/all_gather | solution.py:88
  605.6 44.3 %all-gather.23.cloned.1.call-done = bf16[768,1536]{1,0:T(8,128)(2,1)} async-done(((bf16[192,1536]{1,0:T(8,128)(2,1)}), bf16[768,1536]{1,0:T(8,128)(2,1)}) %all-gather.23.cloned.1.call-update) | async-done | bytes 2359312 | tf_op jit(solution)/shard_map/all_gather | solution.py:88
  656.4 27.5 %reduce-scatter.14.cloned.1.call-done = bf16[192,1536]{1,0:T(8,128)(2,1)} async-done(((bf16[768,1536]{1,0:T(8,128)(2,1)}), bf16[192,1536]{1,0:T(8,128)(2,1)}) %reduce-scatter.14.cloned.1.call-update) | async-done | bytes 589840 | tf_op jit(solution)/shard_map/reduce_scatter | solution.py:101
  692.3 16.4 %collective-permute-done.8 = f32[6144]{0:T(1024)S(1)} collective-permute-done((f32[6144]{0:T(1024)S(1)}, f32[6144]{0:T(1024)S(1)}, u32[]{:S(2)}, u32[]{:S(2)}) %collective-permute-start.8) | collective-permute-done | bytes 24608 | tf_op jit(solution)/shard_map/ppermute | solution.py:97
  758.0 9.7 all-reduce
  767.7 135.5 %psum.39 = f32[1536]{0:T(1024)} all-reduce(f32[1536]{0:T(1024)S(1)} %get-tuple-element.5), channel_id=1, replica_groups=mesh['dp'=2,'row'=4,'col'=4] {'dp','col'}, use_global_device_ids=true, to_apply=%region_18.0 | all-reduce | flops 1536 | bytes 12288 | tf_op jit(solution)/shard_map/psum | solution.py:111
  921.3 36.6 %collective-permute-done.3 = bf16[768,1536]{1,0:T(8,128)(2,1)S(1)} collective-permute-done((bf16[768,1536]{1,0:T(8,128)(2,1)S(1)}, bf16[768,1536]{1,0:T(8,128)(2,1)S(1)}, u32[]{:S(2)}, u32[]{:S(2)}) %collective-permute-start.3) | collective-permute-done | bytes 2359328 | tf_op jit(solution)/shard_map/ppermute | solution.py:66
  (138 shorter events, 148.3 us)
Async XLA Ops:
  7.2 29.2 %all-gather.11.cloned.1.call-start = ((), (), s32[]{:S(2)}) async-start(), calls=%async_computation.5 | async-start | bytes 2949120 | tf_op jit(solution)/shard_map/all_gather | solution.py:40
  7.9 84.6 %reduce-scatter.10.cloned.1.call-start = ((), (), s32[]{:S(2)}) async-start(), calls=%async_computation.10 | async-start | bytes 2949120 | tf_op jit(solution)/shard_map/reduce_scatter | solution.py:82
  44.7 97.8 %reduce-scatter.12.cloned.1.call-start = ((), (), s32[]{:S(2)}) async-start(), calls=%async_computation.12 | async-start | bytes 2949120 | tf_op jit(solution)/shard_map/reduce_scatter | solution.py:82
  53.7 138.0 %reduce-scatter.6.cloned.1.call-start = ((), (), s32[]{:S(2)}) async-start(), calls=%async_computation.6 | async-start | bytes 2949120 | tf_op jit(solution)/shard_map/reduce_scatter | solution.py:82
  61.3 179.8 %reduce-scatter.8.cloned.1.call-start = ((), (), s32[]{:S(2)}) async-start(), calls=%async_computation.8 | async-start | bytes 2949120 | tf_op jit(solution)/shard_map/reduce_scatter | solution.py:82
  68.8 227.6 %all-gather.13.cloned.1.call-start = ((), (), s32[]{:S(2)}) async-start(), calls=%async_computation.7 | async-start | bytes 2949120 | tf_op jit(solution)/shard_map/all_gather | solution.py:90
  246.8 100.5 %all-gather.17.cloned.1.call-start = ((), (), s32[]{:S(2)}) async-start(), calls=%async_computation.11 | async-start | bytes 2949120 | tf_op jit(solution)/shard_map/all_gather | solution.py:90
  247.5 150.0 %all-gather.15.cloned.1.call-start = ((), (), s32[]{:S(2)}) async-start(), calls=%async_computation.9 | async-start | bytes 2949120 | tf_op jit(solution)/shard_map/all_gather | solution.py:90
  248.3 199.6 %all-gather.19.cloned.1.call-start = ((), (), s32[]{:S(2)}) async-start(), calls=%async_computation.13 | async-start | bytes 2949120 | tf_op jit(solution)/shard_map/all_gather | solution.py:90
  249.0 249.4 %all-gather.29.cloned.1.call-start = ((), (), s32[]{:S(2)}) async-start(), calls=%async_computation.19 | async-start | bytes 2949120 | tf_op jit(solution)/shard_map/all_gather | solution.py:88
  249.6 299.1 %all-gather.27.cloned.1.call-start = ((), (), s32[]{:S(2)}) async-start(), calls=%async_computation.18 | async-start | bytes 2949120 | tf_op jit(solution)/shard_map/all_gather | solution.py:88
  250.4 348.6 %all-gather.25.cloned.1.call-start = ((), (), s32[]{:S(2)}) async-start(), calls=%async_computation.17 | async-start | bytes 2949120 | tf_op jit(solution)/shard_map/all_gather | solution.py:88
  250.9 398.9 %all-gather.23.cloned.1.call-start = ((), (), s32[]{:S(2)}) async-start(), calls=%async_computation.16 | async-start | bytes 2949120 | tf_op jit(solution)/shard_map/all_gather | solution.py:88
  251.7 432.2 %reduce-scatter.14.cloned.1.call-start = ((), (), s32[]{:S(2)}) async-start(), calls=%async_computation.14 | async-start | bytes 2949120 | tf_op jit(solution)/shard_map/reduce_scatter | solution.py:101
  460.6 274.2 %all-gather.21.cloned.1.call-start = ((), (), s32[]{:S(2)}) async-start(), calls=%async_computation.15 | async-start | bytes 2949120 | tf_op jit(solution)/shard_map/all_gather | solution.py:49
  503.5 205.9 %collective-permute-start.7 = (bf16[1536,768]{1,0:T(8,128)(2,1)}, bf16[1536,768]{1,0:T(8,128)(2,1)}, u32[]{:S(2)}, u32[]{:S(2)}) collective-permute-start(bf16[1536,768]{1,0:T(8,128)(2,1)} %convolution_convert_fusion), channel_id=1, source_target_pairs={{0,16},{16,0},{1,17},{17,1},{2,18},{18,2},{3,19},{19,3},{4,20},{20... | collective-permute-start | bytes 7077896 | tf_op jit(solution)/shard_map/ppermute | solution.py:75
  553.9 162.9 %collective-permute-start.6 = (bf16[1536,768]{1,0:T(8,128)(2,1)}, bf16[1536,768]{1,0:T(8,128)(2,1)}, u32[]{:S(2)}, u32[]{:S(2)}) collective-permute-start(bf16[1536,768]{1,0:T(8,128)(2,1)} %convolution_convert_fusion.1), channel_id=1, source_target_pairs={{0,16},{16,0},{1,17},{17,1},{2,18},{18,2},{3,19},{19,3},{4,20},{20... | collective-permute-start | bytes 7077896 | tf_op jit(solution)/shard_map/ppermute | solution.py:75
  604.1 118.7 %collective-permute-start.5 = (bf16[1536,768]{1,0:T(8,128)(2,1)}, bf16[1536,768]{1,0:T(8,128)(2,1)}, u32[]{:S(2)}, u32[]{:S(2)}) collective-permute-start(bf16[1536,768]{1,0:T(8,128)(2,1)} %convolution_convert_fusion.2), channel_id=1, source_target_pairs={{0,16},{16,0},{1,17},{17,1},{2,18},{18,2},{3,19},{19,3},{4,20},{20... | collective-permute-start | bytes 7077896 | tf_op jit(solution)/shard_map/ppermute | solution.py:75
  655.0 73.9 %collective-permute-start.4 = (bf16[1536,768]{1,0:T(8,128)(2,1)}, bf16[1536,768]{1,0:T(8,128)(2,1)}, u32[]{:S(2)}, u32[]{:S(2)}) collective-permute-start(bf16[1536,768]{1,0:T(8,128)(2,1)} %convolution_convert_fusion.3), channel_id=1, source_target_pairs={{0,16},{16,0},{1,17},{17,1},{2,18},{18,2},{3,19},{19,3},{4,20},{20... | collective-permute-start | bytes 7077896 | tf_op jit(solution)/shard_map/ppermute | solution.py:75
  690.8 18.0 %collective-permute-start.8 = (f32[6144]{0:T(1024)S(1)}, f32[6144]{0:T(1024)S(1)}, u32[]{:S(2)}, u32[]{:S(2)}) collective-permute-start(f32[6144]{0:T(1024)S(1)} %pad_maximum_fusion.2), channel_id=1, source_target_pairs={{0,16},{16,0},{1,17},{17,1},{2,18},{18,2},{3,19},{19,3},{4,20},{20... | collective-permute-start | bytes 73736 | tf_op jit(solution)/shard_map/ppermute | solution.py:97
  740.3 169.2 %collective-permute-start = (bf16[768,1536]{1,0:T(8,128)(2,1)}, bf16[768,1536]{1,0:T(8,128)(2,1)}, u32[]{:S(2)}, u32[]{:S(2)}) collective-permute-start(bf16[768,1536]{1,0:T(8,128)(2,1)} %convolution_convert_fusion.7), channel_id=1, source_target_pairs={{0,16},{16,0},{1,17},{17,1},{2,18},{18,2},{3,19},{19,3},{4,20},{20... | collective-permute-start | bytes 7077896 | tf_op jit(solution)/shard_map/ppermute | solution.py:66
  745.3 168.1 %collective-permute-start.1 = (bf16[768,1536]{1,0:T(8,128)(2,1)}, bf16[768,1536]{1,0:T(8,128)(2,1)}, u32[]{:S(2)}, u32[]{:S(2)}) collective-permute-start(bf16[768,1536]{1,0:T(8,128)(2,1)} %convolution_convert_fusion.6), channel_id=1, source_target_pairs={{0,16},{16,0},{1,17},{17,1},{2,18},{18,2},{3,19},{19,3},{4,20},{20... | collective-permute-start | bytes 7077896 | tf_op jit(solution)/shard_map/ppermute | solution.py:66
  749.3 168.0 %collective-permute-start.2 = (bf16[768,1536]{1,0:T(8,128)(2,1)}, bf16[768,1536]{1,0:T(8,128)(2,1)}, u32[]{:S(2)}, u32[]{:S(2)}) collective-permute-start(bf16[768,1536]{1,0:T(8,128)(2,1)} %convolution_convert_fusion.5), channel_id=1, source_target_pairs={{0,16},{16,0},{1,17},{17,1},{2,18},{18,2},{3,19},{19,3},{4,20},{20... | collective-permute-start | bytes 7077896 | tf_op jit(solution)/shard_map/ppermute | solution.py:66
  907.5 50.4 %collective-permute-start.3 = (bf16[768,1536]{1,0:T(8,128)(2,1)S(1)}, bf16[768,1536]{1,0:T(8,128)(2,1)S(1)}, u32[]{:S(2)}, u32[]{:S(2)}) collective-permute-start(bf16[768,1536]{1,0:T(8,128)(2,1)S(1)} %convolution_convert_fusion.4), channel_id=1, source_target_pairs={{0,16},{16,0},{1,17},{17,1},{2,18},{18,2},{3,19},{19,3},{4,20},{20... | collective-permute-start | bytes 7077896 | tf_op jit(solution)/shard_map/ppermute | solution.py:66
  (27 other events, 472.9 us)
Sparse Core Ops, SparseCore 0:
  9.5 26.7 all-gather.10
  44.8 47.6 reduce-scatter.9
  95.4 47.0 reduce-scatter.11
  144.7 47.0 reduce-scatter.5
  193.9 47.0 reduce-scatter.7
  246.9 49.3 all-gather.12
  298.5 48.7 all-gather.16
  348.8 48.7 all-gather.14
  399.2 48.7 all-gather.18
  449.4 48.9 all-gather.28
  500.0 48.7 all-gather.26
  550.2 48.7 all-gather.24
  601.1 48.7 all-gather.22
  652.3 31.5 reduce-scatter.13
  686.6 24.0 all-gather.20
